TPU v7x, 128 devices: a whole 4x4x4 slice. The times are simulated.
128 devices in a mesh: rows: 8 (over z, x_lo), cols: 16 (over y, x_hi, core).
Axes of the slice: x: 4 (x_hi: 2, x_lo: 2; x = x_hi * 2 + x_lo), y: 4, z: 4, core: 2. Of those that a mesh axis runs over, the one named last changes fastest.
Arguments:
- global_in: bfloat16 [16, 64, 1024], P('rows', None, 'cols'), may hold values from -6 to 6
- global_first: bfloat16 [3, 3, 1024, 1024], P(None, None, None, 'cols'), may hold values from -0.0625 to 0.0625
- global_second: bfloat16 [3, 3, 1024, 1024], P(None, None, None, 'cols'), may hold values from -0.0625 to 0.0625
- project_weight: bfloat16 [1024, 128], replicated, may hold values from -0.1875 to 0.1875
- enhancer_input: bfloat16 [256, 1024, 128], P('rows', 'cols'), may hold values from -6 to 6
- instance_map: int32 [256, 1024], P('rows', 'cols'), may hold values from 0 to 255, as said below
- encoder_features: float32 [16, 256, 1024], P(None, 'rows', 'cols'), may hold values from -5 to 5
- instance_weight: float32 [16, 128], replicated, may hold values from -4 to 4
- enhancer_first: bfloat16 [3, 3, 128, 128], replicated, may hold values from -0.1875 to 0.1875
- enhancer_second: bfloat16 [3, 3, 128, 128], replicated, may hold values from -0.1875 to 0.1875
- output_cotangent: bfloat16 [256, 1024, 128], P('rows', 'cols'), may hold values from -6 to 6
Outputs:
- enhanced: bfloat16 [256, 1024, 128], P('rows', 'cols')
- gradient_first: float32 [3, 3, 128, 128], replicated
- gradient_second: float32 [3, 3, 128, 128], replicated
- global_gradient: float32 [16, 64, 128], P('rows', 'cols')
Inputs may be any that keep to these rules, and one draw needn't show every extreme that they name: `instance_map`: constant on each aligned 16 x 16 block of fine pixels.
All inputs are finite; a program needn't handle non-finite values.
Results may differ from a plain program's by a relative error of at most 0.0075.
Values may be sent and summed in bfloat16 or wider, within the bound.
A program may use at most 64 MiB of HBM per device.

v0:
```python
import functools
import math

import jax
import jax.numpy as jnp
from jax import lax
from jax.experimental import pallas as pl
from jax.experimental.pallas import tpu as pltpu
from jax.sharding import PartitionSpec as P

MESH = pl.DeviceIdType.MESH
HIGH = lax.Precision.HIGHEST
F32 = jnp.float32
BF16 = jnp.bfloat16
EPS = 1e-05
LABELS = 256
UP = 16
W = 80


class Flow:
    def __init__(self, start, wait):
        self.start = start
        self.wait = wait


def mm(a, b):
    return jnp.dot(a, b, preferred_element_type=F32)


def mm_t0(a, b, **kw):
    return lax.dot_general(a, b, (((0,), (0,)), ((), ())), preferred_element_type=F32, **kw)


def mm_t1(a, b, **kw):
    return lax.dot_general(a, b, (((1,), (1,)), ((), ())), preferred_element_type=F32, **kw)


def kernel(
    nr,
    nc,
    gin_hbm,
    gw1_hbm,
    gw2_hbm,
    pw_hbm,
    ein,
    imap_hbm,
    feats_hbm,
    iw_hbm,
    w1_hbm,
    w2_hbm,
    cot,
    enh_out,
    g1_out,
    g2_out,
    gg_out,
    gin,
    gw1,
    gw2,
    pw,
    imap,
    feats,
    iw,
    w1,
    w2,
    bd,
    gsend,
    gbuf,
    hbuf,
    hsend,
    xcat,
    zs,
    psend,
    precv,
    ssend,
    sbuf,
    gop,
    gos,
    gob,
    csend,
    crecv,
    einp,
    cotp,
    pbuf,
    pall,
    nsend,
    nbp,
    ringp,
    fsend,
    fbuf,
    m3,
    a3,
    c3,
    cott,
    fgt,
    w2t,
    fa,
    ag,
    tsend,
    tcol,
    tsum,
    trow,
    gacc,
    gpair,
    ghalf,
    gcol,
    gred,
    grow,
    gfin,
    gall,
    local_sem,
    ring_s,
    ring_r,
    fwd_s,
    fwd_r,
    col_s,
    col_r,
    row_s,
    row_r,
    nb_s,
    nb_r,
):
    r = lax.axis_index("rows")
    c = lax.axis_index("cols")
    chips = nc // 2
    chip = c // 2
    core = lax.rem(c, 2)

    def remote(src, dst, ss, rs, dev):
        return pltpu.make_async_remote_copy(
            src_ref=src, dst_ref=dst, send_sem=ss, recv_sem=rs, device_id=dev, device_id_type=MESH
        )

    def one(i, src, dst, dev):
        copy = remote(src, dst, nb_s.at[i], nb_r.at[i], dev)
        return Flow(copy.start, copy.wait)

    def many(count, copy_of, got, ss, rs):
        def start():
            def body(k, carry):
                copy_of(k).start()
                return carry

            lax.fori_loop(1, count, body, 0)

        def wait():
            pltpu.make_async_copy(got, got, ss).wait()
            pltpu.make_async_copy(got, got, rs).wait()

        return Flow(start, wait)

    def to_cols(n, src_of, dst):
        def copy_of(k):
            t = lax.rem(c + k, nc)
            return remote(src_of(t), dst.at[c], col_s.at[n], col_r.at[n], (r, t))

        return many(nc, copy_of, dst.at[pl.ds(0, nc - 1)], col_s.at[n], col_r.at[n])

    def to_rows(n, src, dst):
        def copy_of(k):
            return remote(src, dst.at[r], row_s.at[n], row_r.at[n], (lax.rem(r + k, nr), c))

        return many(nr, copy_of, dst.at[pl.ds(0, nr - 1)], row_s.at[n], row_r.at[n])

    def to_chips(n, src_of, dst, got):
        def copy_of(k):
            t = lax.rem(chip + k, chips)
            return remote(src_of(t), dst, ring_s.at[n], ring_r.at[n], (r, 2 * t + core))

        return many(chips, copy_of, got, ring_s.at[n], ring_r.at[n])

    def to_partner(n, src, dst):
        copy = remote(src, dst, fwd_s.at[n], fwd_r.at[n], (r, 2 * chip + 1 - core))
        return Flow(copy.start, copy.wait)

    def gather(n, src, dst):
        return (
            to_chips(n, lambda t: src, dst.at[core, chip], dst.at[core, pl.ds(0, chips - 1)]),
            to_partner(n, dst.at[core], dst.at[core]),
        )

    def own_block(src, dst):
        dst[pl.ds(core, 1), pl.ds(chip, 1)] = src[...][None, None]

    def wrap_r(d):
        return lax.rem(r + d + nr, nr)

    def wrap_c(d):
        return lax.rem(c + d + nc, nc)

    pairs = {
        "gin": (gin_hbm, gin),
        "feats": (feats_hbm, feats),
        "imap": (imap_hbm, imap),
        "gw1": (gw1_hbm, gw1),
        "w2": (w2_hbm, w2),
        "cot": (cot, cotp.at[pl.ds(2, 32), pl.ds(0, 64)]),
        "iw": (iw_hbm, iw),
        "gw2": (gw2_hbm, gw2),
        "pw": (pw_hbm, pw),
        "ein": (ein, einp.at[pl.ds(2, 32), pl.ds(0, 64)]),
        "w1": (w1_hbm, w1),
    }
    own = {
        name: pltpu.make_async_copy(src, dst, local_sem.at[i])
        for i, (name, (src, dst)) in enumerate(pairs.items())
    }
    for copy in own.values():
        copy.start()

    barrier = pltpu.get_barrier_semaphore()

    def greet(dr, dc):
        pl.semaphore_signal(barrier, inc=1, device_id=(wrap_r(dr), lax.rem(c + dc, nc)), device_id_type=MESH)

    def greet_cols(k, carry):
        greet(0, k)
        return carry

    def greet_rows(k, carry):
        greet(k, 0)
        return carry

    lax.fori_loop(1, nc, greet_cols, 0)
    lax.fori_loop(1, nr, greet_rows, 0)

    own["gin"].wait()
    gsend[:, 0:64] = gin[0:64, :]
    gsend[:, 64:128] = gin[64:128, :]

    own["feats"].wait()
    own["imap"].wait()
    lane8 = lax.broadcasted_iota(jnp.int32, (8, 64), 1)
    row8 = lax.broadcasted_iota(jnp.int32, (8, 64), 0)
    packed = jnp.zeros((8, 16), F32)
    label = jnp.zeros((8, 1), F32)
    for br in range(2):
        strip = jnp.sum(feats[:, br * UP : (br + 1) * UP, :], axis=1)
        pick = ((lane8 // UP == row8 % 4) & (row8 // 4 == br)).astype(F32)
        packed = packed + mm_t1(pick, strip, precision=HIGH)
        corner = ((lane8 == UP * (row8 % 4)) & (row8 // 4 == br)).astype(F32)
        line = imap[br * UP : br * UP + 1, :].astype(F32)
        label = label + jnp.sum(corner * line, axis=1, keepdims=True)
    pbuf[...] = jnp.zeros_like(pbuf)
    pbuf[:, 0:16] = packed
    pbuf[:, 16:17] = jnp.full((8, 1), float(UP * UP), F32)
    pbuf[:, 17:18] = label

    pl.semaphore_wait(barrier, nc - 1 + nr - 1)

    first_in, first_fwd = gather(0, gsend, gbuf)
    first_in.start()
    own_block(gsend, gbuf)
    sums_in, sums_fwd = gather(1, pbuf, pall)
    sums_in.start()
    own_block(pbuf, pall)

    def halo(i, src, dst):
        rows32 = pl.ds(2, 32)
        sides = [
            one(4 * i, src.at[:, pl.ds(0, 8)], dst.at[rows32, pl.ds(64, 8)], (r, wrap_c(-1))),
            one(4 * i + 1, src.at[:, pl.ds(56, 8)], dst.at[rows32, pl.ds(72, 8)], (r, wrap_c(1))),
        ]
        ends = [
            one(4 * i + 2, dst.at[pl.ds(2, 2)], dst.at[pl.ds(34, 2)], (wrap_r(-1), c)),
            one(4 * i + 3, dst.at[pl.ds(32, 2)], dst.at[pl.ds(0, 2)], (wrap_r(1), c)),
        ]
        return sides, ends

    cot_sides, cot_ends = halo(0, cot, cotp)
    ein_sides, ein_ends = halo(1, ein, einp)
    for flow in cot_sides:
        flow.start()

    own["w2"].wait()
    for a in range(3):
        for b in range(3):
            w2t[a, b * 128 : (b + 1) * 128, :] = (
                w2[2 - a, (2 - b) * 128 : (3 - b) * 128, :].astype(F32).T.astype(BF16)
            )
    own["pw"].wait()
    bd[...] = jnp.zeros_like(bd)
    for k in range(nc):
        bd[k, 0:64, 0:128] = pw[k * 64 : (k + 1) * 64, :]
        bd[k, 64:128, 128:256] = pw[k * 64 : (k + 1) * 64, :]

    col80 = lax.broadcasted_iota(jnp.int32, (W, 128), 0)
    colown = col80 < 64
    colmap = colown | ((col80 < 72) & (c < nc - 1)) | ((col80 >= 72) & (c > 0))

    def shifts(value):
        return jnp.concatenate(
            [
                pltpu.roll(value, 1, 0).astype(BF16),
                value.astype(BF16),
                pltpu.roll(value, W - 1, 0).astype(BF16),
            ],
            axis=1,
        )

    def in_map(i, first, last):
        return colmap & ((i >= first) | (r > 0)) & ((i <= last) | (r < nr - 1))

    map_sums = to_rows(0, fsend, fbuf)
    near = [
        one(8, nsend, nbp.at[2], (wrap_r(-1), c)),
        one(9, nsend, nbp.at[0], (wrap_r(1), c)),
    ]

    def window_1():
        sums_fwd.wait()
        band_p = pall[...].reshape(8 * nc, 128)
        hot = (
            lax.broadcasted_iota(jnp.int32, (8 * nc, LABELS), 1)
            == band_p[:, 17:18].astype(jnp.int32)
        ).astype(F32)
        fsend[...] = mm_t0(band_p, hot, precision=HIGH)[0:24, :]
        map_sums.start()
        fbuf[pl.ds(r, 1)] = fsend[...][None]
        nsend[1] = pbuf[...]
        for i, t in ((0, wrap_c(-1)), (2, wrap_c(1))):
            nsend[pl.ds(i, 1)] = pall[pl.ds(lax.rem(t, 2), 1), pl.ds(t // 2, 1)][0]
        nbp[1] = nsend[...]
        for flow in near:
            flow.start()
        own["cot"].wait()
        for flow in cot_sides:
            flow.wait()
        for flow in cot_ends:
            flow.start()

    def band_conv(buf, w, n, window):
        for k in range(nc):
            block = buf[k % 2, k // 2]
            xcat[0:64, k * 64 : (k + 1) * 64] = block[:, 0:64]
            xcat[64:128, k * 64 : (k + 1) * 64] = block[:, 64:128]
        j = lax.broadcasted_iota(jnp.int32, (128, 64), 0) % 64
        z = mm_t1(xcat[...], w[...].reshape(576, 1024))
        zs[8:136, :] = z
        out = []
        for a in range(3):
            t = a * 192
            before = jnp.where(j > 0, zs[7:135, t : t + 64], 0.0)
            after = jnp.where(j < 63, zs[9:137, t + 128 : t + 192], 0.0)
            out.append(before + z[:, t + 64 : t + 128] + after)
        for half in range(2):
            psend[n, 0, :, half * 64 : half * 64 + 64] = out[2][32 * half : 32 * half + 32]
            psend[n, 1, :, half * 64 : half * 64 + 64] = out[0][64 + 32 * half : 96 + 32 * half]
        up = one(10 + 2 * n, psend.at[n, 0], precv.at[n, 1], (wrap_r(-1), c))
        down = one(11 + 2 * n, psend.at[n, 1], precv.at[n, 0], (wrap_r(1), c))
        up.start()
        down.start()
        top = out[1][0:64] + out[2][64:128]
        low = out[0][0:64] + out[1][64:128]
        window()
        up.wait()
        down.wait()
        came = [
            jnp.concatenate([precv[n, i, :, 0:64], precv[n, i, :, 64:128]], axis=0)
            for i in range(2)
        ]
        top = top + jnp.where(r > 0, came[0], 0.0)
        low = low + jnp.where(r < nr - 1, came[1], 0.0)
        return jnp.concatenate([top, low], axis=0)

    zs[...] = jnp.zeros_like(zs)
    first_in.wait()
    first_fwd.start()
    sums_in.wait()
    sums_fwd.start()
    own["gw1"].wait()
    first_fwd.wait()
    first_raw = band_conv(gbuf, gw1, 0, window_1)
    ssend[...] = jnp.zeros_like(ssend)
    ssend[0:1, 0:64] = jnp.sum(first_raw, 0, keepdims=True)
    ssend[1:2, 0:64] = jnp.sum(first_raw * first_raw, 0, keepdims=True)
    band_stats = to_rows(1, ssend, sbuf)
    band_stats.start()
    sbuf[pl.ds(r, 1)] = ssend[...][None]
    for flow in ein_sides:
        flow.start()
    band_stats.wait()
    sums = jnp.sum(sbuf[...], axis=0)[:, 0:64]
    band_total = float(nr * 128)
    band_mean = sums[0:1, :] / band_total
    band_var = sums[1:2, :] / band_total - band_mean * band_mean
    normed = (first_raw - band_mean) * lax.rsqrt(band_var + EPS)
    hidden = jnp.maximum(normed, 0.0).astype(BF16)
    hsend[:, 0:64] = hidden[0:64]
    hsend[:, 64:128] = hidden[64:128]
    hidden_in, hidden_fwd = gather(2, hsend, hbuf)
    hidden_in.start()
    own_block(hsend, hbuf)

    for flow in cot_ends:
        flow.wait()
    own["ein"].wait()
    for flow in ein_sides:
        flow.wait()

    def cot_row(i, carry):
        value = jnp.where(in_map(i, 2, 33), cotp[i].astype(F32), 0.0)
        c3[i] = shifts(value)
        return carry

    lax.fori_loop(0, 36, cot_row, 0)

    def cot_turn(q, carry):
        value = cotp[pl.ds(2 + 8 * q, 8), 0:64, :].astype(F32)
        cott[q] = value.reshape(512, 128).T.astype(BF16)
        return carry

    lax.fori_loop(0, 4, cot_turn, 0)

    hidden_in.wait()
    hidden_fwd.start()
    for flow in ein_ends:
        flow.start()
    map_sums.wait()
    for flow in near:
        flow.wait()
    fsum = jnp.sum(fbuf[...], axis=0)
    averages = fsum[0:16, :] / jnp.maximum(fsum[16:17, :], 1.0)
    ringp[...] = jnp.zeros_like(ringp)
    for br in range(4):
        dr, their_br = {0: (0, 1), 1: (1, 0), 2: (1, 1), 3: (2, 0)}[br]
        for q in range(6):
            dc, their_bc = (0, 3) if q == 0 else (2, 0) if q == 5 else (1, q - 1)
            p = their_br * 4 + their_bc
            ringp[br * 8 + q : br * 8 + q + 1, :] = nbp[dr, dc, p : p + 1, :]
    ring_hot = (
        lax.broadcasted_iota(jnp.int32, (32, LABELS), 1) == ringp[:, 17:18].astype(jnp.int32)
    ).astype(F32)
    own["iw"].wait()
    ring_avg = mm_t1(ring_hot, averages, precision=HIGH)
    pooled = jnp.dot(ring_avg, iw[...], precision=HIGH, preferred_element_type=F32)

    own["gw2"].wait()
    hidden_fwd.wait()
    second_raw = band_conv(hbuf, gw2, 1, lambda: None)
    global_out = (gin[...].astype(F32) + second_raw).astype(BF16).astype(F32)
    gop[...] = jnp.zeros_like(gop)
    gop[8:72, 0:64] = global_out[0:64]
    gop[8:72, 64:128] = global_out[64:128]
    for t in range(nc):
        gos[t] = gop[4 * t + 7 : 4 * t + 15, :]

    spread_out = to_cols(0, lambda t: gos.at[t], gob)
    spread_out.start()
    gob[pl.ds(c, 1)] = gos[pl.ds(c, 1)]
    for flow in ein_ends:
        flow.wait()
    spread_out.wait()
    packets = jnp.concatenate([gob[k].astype(BF16) for k in range(nc)], axis=1)
    both = mm(packets, bd[...].reshape(nc * 128, 256)).astype(BF16).astype(F32)
    csend[0] = both[:, 0:128]
    csend[1] = both[:, 128:256]
    edges = [
        one(14, csend.at[0], crecv.at[1], (wrap_r(-1), c)),
        one(15, csend.at[1], crecv.at[0], (wrap_r(1), c)),
    ]
    for flow in edges:
        flow.start()

    def mix_rows(br, coarse, start, stop):
        terms = coarse + pooled[br * 8 : br * 8 + 8]
        pieces = []
        for q in (1, 2, 3, 4, 5, 0):
            line = terms[q : q + 1, :]
            pieces.append(jnp.broadcast_to(line, (8 if q in (0, 5) else UP, 128)))
        add = jnp.concatenate(pieces, axis=0)

        def mix_row(i, carry):
            value = einp[i].astype(F32) + add
            value = jnp.where(in_map(i, 2, 33), value, 0.0).astype(BF16).astype(F32)
            m3[i] = shifts(value)
            return carry

        lax.fori_loop(start, stop, mix_row, 0)

    mix_rows(1, both[:, 0:128], 2, 18)
    mix_rows(2, both[:, 128:256], 18, 34)
    own["w1"].wait()

    def conv_part(src, w, first, count):
        width = src.shape[1]
        x = jnp.concatenate(
            [src[first + a : first + a + count].reshape(count * width, 384) for a in range(3)],
            axis=1,
        )
        return mm(x, w[...].reshape(1152, 128)).reshape(count, width, 128)

    fa[2:17] = conv_part(m3, w1, 2, 15)
    fa[17:32] = conv_part(m3, w1, 17, 15)
    for flow in edges:
        flow.wait()
    mix_rows(0, crecv[0], 0, 2)
    mix_rows(3, crecv[1], 34, 36)
    fa[0:2] = conv_part(m3, w1, 0, 2)
    fa[32:34] = conv_part(m3, w1, 32, 2)

    tile_cols = [to_cols(1 + n, lambda t, n=n: tsend.at[n], tcol.at[n]) for n in range(2)]
    tile_rows = [to_rows(2 + n, tsum.at[n], trow.at[n]) for n in range(2)]

    def tile_sums(n, x, y):
        tsend[n] = jnp.zeros((8, 128), F32)
        tsend[n, 0:1, :] = jnp.sum(x, axis=(0, 1))[None]
        tsend[n, 1:2, :] = jnp.sum(y, axis=(0, 1))[None]
        tile_cols[n].start()
        tcol[n, pl.ds(c, 1)] = tsend[n][None]

    def tile_sums_2(n):
        tile_cols[n].wait()
        tsum[n] = jnp.sum(tcol[n], axis=0)
        tile_rows[n].start()
        trow[n, pl.ds(r, 1)] = tsum[n][None]

    def tile_sums_3(n):
        tile_rows[n].wait()
        return jnp.sum(trow[n], axis=0)

    act = fa[1:33, 0:64, :]
    tile_sums(0, act, act * act)
    ag[0:17] = conv_part(c3, w2t, 0, 17)
    tile_sums_2(0)
    ag[17:34] = conv_part(c3, w2t, 17, 17)
    sums = tile_sums_3(0)
    pixels = float(nr * nc * 2048)
    act_mean = sums[0:1, :] / pixels
    inverse_dev = lax.rsqrt(sums[1:2, :] / pixels - act_mean * act_mean + EPS)

    def act_row(i, carry):
        na = (fa[i] - act_mean) * inverse_dev
        s = jax.nn.sigmoid(na)
        fa[i] = na
        ng = ag[i] * s * (1.0 + na * (1.0 - s))
        ag[i] = ng
        value = jnp.where(in_map(i, 1, 32), na * s, 0.0).astype(BF16).astype(F32)
        a3[i] = shifts(value)[0:64]
        return carry

    lax.fori_loop(0, 34, act_row, 0)
    ng = ag[1:33, 0:64, :]
    tile_sums(1, ng, ng * fa[1:33, 0:64, :])

    def weight_part(n, turned, src, first):
        for a in range(3):
            got = jnp.zeros((128, 384), F32)
            for q in range(4):
                start = first + a + 8 * q
                rhs = src[start : start + 8, 0:64, :].reshape(512, 384)
                got = got + mm(turned[q], rhs)
            for b in range(3):
                gacc[n, a * 384 + b * 128 : a * 384 + (b + 1) * 128, :] = got[
                    :, b * 128 : (b + 1) * 128
                ].T

    half_rows = 1152 // 2
    chunk = half_rows // chips

    def half_of(h):
        return pl.ds(pl.multiple_of(h * half_rows, 16), half_rows)

    def piece(h, q):
        return pl.ds(pl.multiple_of(h * half_rows + q * chunk, 8), chunk)

    pair_sum = [to_partner(3 + n, gacc.at[n, half_of(1 - core)], gpair.at[n]) for n in range(2)]
    band_sum = [
        to_chips(
            3 + n,
            lambda t, n=n: ghalf.at[n, t],
            gcol.at[n, chip],
            gcol.at[n, pl.ds(0, chips - 1)],
        )
        for n in range(2)
    ]
    map_sum = [to_rows(4 + n, gred.at[n], grow.at[n]) for n in range(2)]
    share = [
        to_chips(
            5 + n,
            lambda t, n=n: gfin.at[n],
            gall.at[n, core, chip],
            gall.at[n, core, pl.ds(0, chips - 1)],
        )
        for n in range(2)
    ]
    share_fwd = [to_partner(5 + n, gall.at[n, core], gall.at[n, core]) for n in range(2)]

    def grad_0(n):
        pair_sum[n].start()

    def grad_1(n):
        pair_sum[n].wait()
        total = gacc[n, half_of(core)] + gpair[n]
        ghalf[n] = total.astype(BF16).reshape(chips, chunk, 128)
        band_sum[n].start()
        gcol[n, pl.ds(chip, 1)] = ghalf[n, pl.ds(chip, 1)]

    def grad_2(n):
        band_sum[n].wait()
        gred[n] = jnp.sum(gcol[n].astype(F32), axis=0)
        map_sum[n].start()
        grow[n, pl.ds(r, 1)] = gred[n][None]

    def grad_3(n):
        map_sum[n].wait()
        total = jnp.sum(grow[n], axis=0)
        gfin[n] = (total * (1.0 / math.sqrt(pixels))).astype(BF16)
        share[n].start()
        gall[n, pl.ds(core, 1), pl.ds(chip, 1)] = gfin[n][None, None]

    def grad_4(n):
        share[n].wait()
        share_fwd[n].start()

    def grad_5(n, out):
        share_fwd[n].wait()
        out[...] = gall[n].reshape(1152, 128).astype(F32)

    weight_part(1, cott, a3, 0)
    grad_0(1)
    tile_sums_2(1)
    for half in range(2):
        got = conv_part(a3, w2, 16 * half, 16)
        enh_out[16 * half : 16 * half + 16] = (
            m3[2 + 16 * half : 18 + 16 * half, 0:64, 128:256].astype(F32) + got
        ).astype(BF16)
        if half == 0:
            grad_1(1)
    sums = tile_sums_3(1)
    grad_mean = sums[0:1, :] / pixels
    cross_mean = sums[1:2, :] / pixels
    grad_2(1)

    def grad_row(i, carry):
        fg = inverse_dev * (ag[i] - grad_mean - fa[i] * cross_mean)
        fg = jnp.where(in_map(i, 1, 32), fg, 0.0).astype(BF16).astype(F32)
        ag[i] = fg

        return carry

    lax.fori_loop(0, 34, grad_row, 0)

    def grad_turn(q, carry):
        value = ag[pl.ds(1 + 8 * q, 8), 0:64, :]
        fgt[q] = value.reshape(512, 128).T.astype(BF16)
        return carry

    lax.fori_loop(0, 4, grad_turn, 0)
    weight_part(0, fgt, m3, 1)
    grad_0(0)
    grad_3(1)
    grad_1(0)

    rows24 = lax.broadcasted_iota(jnp.int32, (24, W), 0)
    cols24 = lax.broadcasted_iota(jnp.int32, (24, W), 1)
    left = UP * (rows24 % 8) + 1 - rows24 // 8
    inside = (cols24 >= left) & (cols24 < left + UP)
    window = ((inside | ((left < 0) & (cols24 == W - 1))) & (rows24 % 8 < 4)).astype(F32)
    picked = [[], [], []]
    direct = []
    for br in range(2):
        total = jnp.sum(ag[UP * br + 1 : UP * br + 17], axis=0)
        below = total - ag[UP * br + 1] + ag[UP * br + 17]
        above = total - ag[UP * br + 16] + ag[UP * br]
        for a, strip in enumerate((below, total, above)):
            picked[a].append(jnp.dot(window, strip, precision=HIGH, preferred_element_type=F32))
        strip = jnp.sum(c3[UP * br + 2 : UP * br + 18, :, 128:256].astype(F32), axis=0)
        direct.append(jnp.dot(window, strip, precision=HIGH, preferred_element_type=F32)[8:16])
    result = jnp.concatenate(direct, axis=0)
    for a in range(3):
        for b in range(3):
            s_ab = jnp.concatenate([picked[a][br][8 * b : 8 * b + 8] for br in range(2)], axis=0)
            result = result + mm_t1(
                s_ab, w1[a, b * 128 : (b + 1) * 128, :].astype(F32), precision=HIGH
            )
    gg_out[0] = result[0:4] * (1.0 / UP)
    gg_out[1] = result[8:12] * (1.0 / UP)

    grad_4(1)
    grad_2(0)
    grad_5(1, g2_out)
    grad_3(0)
    grad_4(0)
    grad_5(0, g1_out)


def hand_over(*refs):
    half = len(refs) // 2
    for source, target in zip(refs[:half], refs[half:]):
        target[...] = source[...]


def per_device(
    nr,
    nc,
    global_in,
    global_first,
    global_second,
    project_weight,
    enhancer_input,
    instance_map,
    encoder_features,
    instance_weight,
    enhancer_first,
    enhancer_second,
    output_cotangent,
):
    vm = pl.BlockSpec(memory_space=pltpu.VMEM)
    hbm = pl.BlockSpec(memory_space=pltpu.HBM)
    chunk = 1152 // nc
    dma = pltpu.SemaphoreType.DMA
    scratch = [
        pltpu.VMEM((128, 64), BF16),
        pltpu.VMEM((9, 64, 1024), BF16),
        pltpu.VMEM((9, 64, 1024), BF16),
        pltpu.VMEM((1024, 128), BF16),
        pltpu.VMEM((32, 64), jnp.int32),
        pltpu.VMEM((16, 32, 64), F32),
        pltpu.VMEM((16, 128), F32),
        pltpu.VMEM((3, 384, 128), BF16),
        pltpu.VMEM((3, 384, 128), BF16),
        pltpu.VMEM((nc, 128, 256), BF16),
        pltpu.VMEM((64, 128), BF16),
        pltpu.VMEM((2, nc // 2, 64, 128), BF16),
        pltpu.VMEM((2, nc // 2, 64, 128), BF16),
        pltpu.VMEM((64, 128), BF16),
        pltpu.VMEM((128, 1024), BF16),
        pltpu.VMEM((144, 576), F32),
        pltpu.VMEM((2, 2, 32, 128), F32),
        pltpu.VMEM((2, 2, 32, 128), F32),
        pltpu.VMEM((8, 128), F32),
        pltpu.VMEM((nr, 8, 128), F32),
        pltpu.VMEM((80, 128), F32),
        pltpu.VMEM((nc, 8, 128), F32),
        pltpu.VMEM((nc, 8, 128), F32),
        pltpu.VMEM((2, 8, 128), F32),
        pltpu.VMEM((2, 8, 128), F32),
        pltpu.VMEM((36, W, 128), BF16),
        pltpu.VMEM((36, W, 128), BF16),
        pltpu.VMEM((8, 128), F32),
        pltpu.VMEM((2, nc // 2, 8, 128), F32),
        pltpu.VMEM((3, 8, 128), F32),
        pltpu.VMEM((3, 3, 8, 128), F32),
        pltpu.VMEM((32, 128), F32),
        pltpu.VMEM((24, LABELS), F32),
        pltpu.VMEM((nr, 24, LABELS), F32),
        pltpu.VMEM((36, W, 384), BF16),
        pltpu.VMEM((34, 64, 384), BF16),
        pltpu.VMEM((36, W, 384), BF16),
        pltpu.VMEM((4, 128, 512), BF16),
        pltpu.VMEM((4, 128, 512), BF16),
        pltpu.VMEM((3, 384, 128), BF16),
        pltpu.VMEM((34, W, 128), F32),
        pltpu.VMEM((34, W, 128), F32),
        pltpu.VMEM((2, 8, 128), F32),
        pltpu.VMEM((2, nc, 8, 128), F32),
        pltpu.VMEM((2, 8, 128), F32),
        pltpu.VMEM((2, nr, 8, 128), F32),
        pltpu.VMEM((2, 1152, 128), F32),
        pltpu.VMEM((2, 576, 128), F32),
        pltpu.VMEM((2, nc // 2, chunk, 128), BF16),
        pltpu.VMEM((2, nc // 2, chunk, 128), BF16),
        pltpu.VMEM((2, chunk, 128), F32),
        pltpu.VMEM((2, nr, chunk, 128), F32),
        pltpu.VMEM((2, chunk, 128), BF16),
        pltpu.VMEM((2, 2, nc // 2, chunk, 128), BF16),
        dma((11,)),
        dma((7,)),
        dma((7,)),
        dma((7,)),
        dma((7,)),
        dma((3,)),
        dma((3,)),
        dma((6,)),
        dma((6,)),
        dma((16,)),
        dma((16,)),
    ]
    enhanced, g1, g2, gg = pl.pallas_call(
        functools.partial(kernel, nr, nc),
        out_shape=(
            jax.ShapeDtypeStruct((32, 64, 128), BF16),
            jax.ShapeDtypeStruct((1152, 128), F32),
            jax.ShapeDtypeStruct((1152, 128), F32),
            jax.ShapeDtypeStruct((2, 4, 128), F32),
        ),
        in_specs=[hbm] * 11,
        out_specs=(vm, vm, vm, vm),
        scratch_shapes=scratch,
        compiler_params=pltpu.CompilerParams(
            collective_id=0, has_side_effects=True, vmem_limit_bytes=44 * 1024 * 1024
        ),
    )(
        *(
            pltpu.with_memory_space_constraint(x, pltpu.HBM)
            for x in (
                global_in.reshape(128, 64),
                jnp.swapaxes(global_first, 2, 3).reshape(9, 64, 1024),
                jnp.swapaxes(global_second, 2, 3).reshape(9, 64, 1024),
                project_weight,
                enhancer_input,
                instance_map,
                encoder_features,
                instance_weight,
                enhancer_first.reshape(3, 384, 128),
                enhancer_second.reshape(3, 384, 128),
                output_cotangent,
            )
        )
    )
    vms = [vm] * 4
    enhanced, g1, g2, gg = pl.pallas_call(
        hand_over,
        out_shape=tuple(jax.ShapeDtypeStruct(x.shape, x.dtype) for x in (enhanced, g1, g2, gg)),
        in_specs=vms,
        out_specs=tuple(vms),
        compiler_params=pltpu.CompilerParams(vmem_limit_bytes=16 * 1024 * 1024),
    )(enhanced, g1, g2, gg)
    return (enhanced, g1.reshape(3, 3, 128, 128), g2.reshape(3, 3, 128, 128), gg)


def solution(mesh):
    nr, nc = mesh.shape["rows"], mesh.shape["cols"]
    return jax.shard_map(
        functools.partial(per_device, nr, nc),
        mesh=mesh,
        in_specs=(
            P("rows", None, "cols"),
            P(None, None, None, "cols"),
            P(None, None, None, "cols"),
            P(),
            P("rows", "cols", None),
            P("rows", "cols"),
            P(None, "rows", "cols"),
            P(),
            P(),
            P(),
            P("rows", "cols", None),
        ),
        out_specs=(P("rows", "cols", None), P(), P(), P("rows", "cols", None)),
        check_vma=False,
    )
```

profile of v0, /device:TPU:1, one launch (start us, length us, event | category | flops | bytes accessed | tf_op | source)
XLA Modules:
  0.0 92.6 jit_solution(9182733927343154009)
XLA Ops:
  0.6 90.7 %shard_map.138 = (bf16[32,64,128]{2,1,0:T(8,128)(2,1)S(1)}, f32[1152,128]{1,0:T(8,128)S(1)}, f32[1152,128]{1,0:T(8,128)S(1)}, f32[2,4,128]{2,1,0:T(4,128)S(1)}) custom-call(bf16[128,64]{1,0:T(8,128)(2,1)} %bitcast.15, bf16[9,64,1024]{2,1,0:T(8,128)(2,1)} %bitcast.11, bf16[9,64,1024]{2,1,0:T(8,128)(2,1)} %bitcast.12, bf16[1024,128]{1,0:T(8,128)(2,1)} %pw_hbm.1, ...), custom_call_target="tpu_custom_call" | custom-call | tf_op jit(solution)/shard_map/pallas_call | solution.py:780
  91.3 1.3 %shard_map.139 = (bf16[32,64,128]{2,1,0:T(8,128)(2,1)}, f32[1152,128]{1,0:T(8,128)}, f32[1152,128]{1,0:T(8,128)}, f32[2,4,128]{2,1,0:T(4,128)}) custom-call(bf16[32,64,128]{2,1,0:T(8,128)(2,1)S(1)} %get-tuple-element.12.refs_0_, f32[1152,128]{1,0:T(8,128)S(1)} %get-tuple-element.13.refs_1_, f32[1152,128]{1,0:T(8,128)S(1)} %get-tuple-element.14.refs_2_, ...), custom_call_target="tpu_custom_call" | custom-call | tf_op jit(solution)/shard_map/pallas_call | solution.py:813
where the time goes:
time: 92.7 us; the launch traced here: 92.6 us
  Pallas kernels  92 us (99%)
    pallas_call x1, Pallas kernels, per_device(): pl.pallas_call(functools.partial(kernel, nr, nc), out_shape=(jax.ShapeDty...  90.7 us

commit v1 on v0

--- a/solution.py
+++ b/solution.py
@@ -307,7 +307,14 @@
         one(9, nsend, nbp.at[0], (wrap_r(1), c)),
     ]
 
-    def window_1():
+    def edge_window():
+        own["cot"].wait()
+        for flow in cot_sides:
+            flow.wait()
+        for flow in cot_ends:
+            flow.start()
+
+    def stats_window():
         sums_fwd.wait()
         band_p = pall[...].reshape(8 * nc, 128)
         hot = (
@@ -322,11 +329,6 @@
             nsend[pl.ds(i, 1)] = pall[pl.ds(lax.rem(t, 2), 1), pl.ds(t // 2, 1)][0]
         nbp[1] = nsend[...]
         for flow in near:
-            flow.start()
-        own["cot"].wait()
-        for flow in cot_sides:
-            flow.wait()
-        for flow in cot_ends:
             flow.start()
 
     def band_conv(buf, w, n, window):
@@ -370,7 +372,7 @@
     sums_fwd.start()
     own["gw1"].wait()
     first_fwd.wait()
-    first_raw = band_conv(gbuf, gw1, 0, window_1)
+    first_raw = band_conv(gbuf, gw1, 0, edge_window)
     ssend[...] = jnp.zeros_like(ssend)
     ssend[0:1, 0:64] = jnp.sum(first_raw, 0, keepdims=True)
     ssend[1:2, 0:64] = jnp.sum(first_raw * first_raw, 0, keepdims=True)
@@ -379,6 +381,7 @@
     sbuf[pl.ds(r, 1)] = ssend[...][None]
     for flow in ein_sides:
         flow.start()
+    stats_window()
     band_stats.wait()
     sums = jnp.sum(sbuf[...], axis=0)[:, 0:64]
     band_total = float(nr * 128)
@@ -416,6 +419,21 @@
     hidden_fwd.start()
     for flow in ein_ends:
         flow.start()
+    own["gw2"].wait()
+    hidden_fwd.wait()
+    second_raw = band_conv(hbuf, gw2, 1, lambda: None)
+    global_out = (gin[...].astype(F32) + second_raw).astype(BF16).astype(F32)
+    gop[...] = jnp.zeros_like(gop)
+    gop[8:72, 0:64] = global_out[0:64]
+    gop[8:72, 64:128] = global_out[64:128]
+    for t in range(nc):
+        gos[t] = gop[4 * t + 7 : 4 * t + 15, :]
+
+    spread_out = to_cols(0, lambda t: gos.at[t], gob)
+    spread_out.start()
+    gob[pl.ds(c, 1)] = gos[pl.ds(c, 1)]
+    for flow in ein_ends:
+        flow.wait()
     map_sums.wait()
     for flow in near:
         flow.wait()
@@ -434,22 +452,6 @@
     own["iw"].wait()
     ring_avg = mm_t1(ring_hot, averages, precision=HIGH)
     pooled = jnp.dot(ring_avg, iw[...], precision=HIGH, preferred_element_type=F32)
-
-    own["gw2"].wait()
-    hidden_fwd.wait()
-    second_raw = band_conv(hbuf, gw2, 1, lambda: None)
-    global_out = (gin[...].astype(F32) + second_raw).astype(BF16).astype(F32)
-    gop[...] = jnp.zeros_like(gop)
-    gop[8:72, 0:64] = global_out[0:64]
-    gop[8:72, 64:128] = global_out[64:128]
-    for t in range(nc):
-        gos[t] = gop[4 * t + 7 : 4 * t + 15, :]
-
-    spread_out = to_cols(0, lambda t: gos.at[t], gob)
-    spread_out.start()
-    gob[pl.ds(c, 1)] = gos[pl.ds(c, 1)]
-    for flow in ein_ends:
-        flow.wait()
     spread_out.wait()
     packets = jnp.concatenate([gob[k].astype(BF16) for k in range(nc)], axis=1)
     both = mm(packets, bd[...].reshape(nc * 128, 256)).astype(BF16).astype(F32)
@@ -625,12 +627,10 @@
         enh_out[16 * half : 16 * half + 16] = (
             m3[2 + 16 * half : 18 + 16 * half, 0:64, 128:256].astype(F32) + got
         ).astype(BF16)
-        if half == 0:
-            grad_1(1)
     sums = tile_sums_3(1)
     grad_mean = sums[0:1, :] / pixels
     cross_mean = sums[1:2, :] / pixels
-    grad_2(1)
+    grad_1(1)
 
     def grad_row(i, carry):
         fg = inverse_dev * (ag[i] - grad_mean - fa[i] * cross_mean)
@@ -649,8 +649,9 @@
     lax.fori_loop(0, 4, grad_turn, 0)
     weight_part(0, fgt, m3, 1)
     grad_0(0)
-    grad_3(1)
+
     grad_1(0)
+    grad_2(1)
 
     rows24 = lax.broadcasted_iota(jnp.int32, (24, W), 0)
     cols24 = lax.broadcasted_iota(jnp.int32, (24, W), 1)
@@ -677,11 +678,12 @@
     gg_out[0] = result[0:4] * (1.0 / UP)
     gg_out[1] = result[8:12] * (1.0 / UP)
 
+    grad_2(0)
+    grad_3(1)
+    grad_3(0)
     grad_4(1)
-    grad_2(0)
+    grad_4(0)
     grad_5(1, g2_out)
-    grad_3(0)
-    grad_4(0)
     grad_5(0, g1_out)
 
 

time: 92.7 us -> 87.9 us (0.948)
  Pallas kernels: 92 us -> 87.2 us
    pallas_call x1, Pallas kernels: 90.7 us -> 85.9 us  [per_device(): pl.pallas_call(functools.partial(kernel, nr, nc), out_shape=(jax.ShapeDty...]
where the time goes in v1:
time: 87.9 us; the launch traced here: 87.8 us
  Pallas kernels  87.2 us (99%)
    pallas_call x1, Pallas kernels, per_device(): pl.pallas_call(functools.partial(kernel, nr, nc), out_shape=(jax.ShapeDty...  85.9 us

profile of v1, /device:TPU:1, one launch (start us, length us, event | category | flops | bytes accessed | tf_op | source)
XLA Modules:
  0.0 87.8 jit_solution(9430983275291586758)
XLA Ops:
  0.6 85.9 %shard_map.138 = (bf16[32,64,128]{2,1,0:T(8,128)(2,1)S(1)}, f32[1152,128]{1,0:T(8,128)S(1)}, f32[1152,128]{1,0:T(8,128)S(1)}, f32[2,4,128]{2,1,0:T(4,128)S(1)}) custom-call(bf16[128,64]{1,0:T(8,128)(2,1)} %bitcast.15, bf16[9,64,1024]{2,1,0:T(8,128)(2,1)} %bitcast.11, bf16[9,64,1024]{2,1,0:T(8,128)(2,1)} %bitcast.12, bf16[1024,128]{1,0:T(8,128)(2,1)} %pw_hbm.1, ...), custom_call_target="tpu_custom_call" | custom-call | tf_op jit(solution)/shard_map/pallas_call | solution.py:782
  86.5 1.3 %shard_map.139 = (bf16[32,64,128]{2,1,0:T(8,128)(2,1)}, f32[1152,128]{1,0:T(8,128)}, f32[1152,128]{1,0:T(8,128)}, f32[2,4,128]{2,1,0:T(4,128)}) custom-call(bf16[32,64,128]{2,1,0:T(8,128)(2,1)S(1)} %get-tuple-element.12.refs_0_, f32[1152,128]{1,0:T(8,128)S(1)} %get-tuple-element.13.refs_1_, f32[1152,128]{1,0:T(8,128)S(1)} %get-tuple-element.14.refs_2_, ...), custom_call_target="tpu_custom_call" | custom-call | tf_op jit(solution)/shard_map/pallas_call | solution.py:815

commit v2 on v1

--- a/solution.py
+++ b/solution.py
@@ -97,9 +97,7 @@
     fa,
     ag,
     tsend,
-    tcol,
-    tsum,
-    trow,
+    tall,
     gacc,
     gpair,
     ghalf,
@@ -117,6 +115,8 @@
     col_r,
     row_s,
     row_r,
+    all_s,
+    all_r,
     nb_s,
     nb_r,
 ):
@@ -161,6 +161,16 @@
             return remote(src, dst.at[r], row_s.at[n], row_r.at[n], (lax.rem(r + k, nr), c))
 
         return many(nr, copy_of, dst.at[pl.ds(0, nr - 1)], row_s.at[n], row_r.at[n])
+
+    def to_all(n, src, dst):
+        me = r * nc + c
+
+        def copy_of(k):
+            t = lax.rem(me + k, nr * nc)
+            return remote(src, dst.at[me], all_s.at[n], all_r.at[n], (t // nc, lax.rem(t, nc)))
+
+        got = dst.at[pl.ds(0, nr * nc - 1)]
+        return many(nr * nc, copy_of, got, all_s.at[n], all_r.at[n])
 
     def to_chips(n, src_of, dst, got):
         def copy_of(k):
@@ -501,32 +511,23 @@
     fa[0:2] = conv_part(m3, w1, 0, 2)
     fa[32:34] = conv_part(m3, w1, 32, 2)
 
-    tile_cols = [to_cols(1 + n, lambda t, n=n: tsend.at[n], tcol.at[n]) for n in range(2)]
-    tile_rows = [to_rows(2 + n, tsum.at[n], trow.at[n]) for n in range(2)]
+    tile_all = [to_all(n, tsend.at[n], tall.at[n]) for n in range(2)]
 
     def tile_sums(n, x, y):
-        tsend[n] = jnp.zeros((8, 128), F32)
         tsend[n, 0:1, :] = jnp.sum(x, axis=(0, 1))[None]
         tsend[n, 1:2, :] = jnp.sum(y, axis=(0, 1))[None]
-        tile_cols[n].start()
-        tcol[n, pl.ds(c, 1)] = tsend[n][None]
+        tile_all[n].start()
+        tall[n, pl.ds(r * nc + c, 1)] = tsend[n][None]
 
     def tile_sums_2(n):
-        tile_cols[n].wait()
-        tsum[n] = jnp.sum(tcol[n], axis=0)
-        tile_rows[n].start()
-        trow[n, pl.ds(r, 1)] = tsum[n][None]
-
-    def tile_sums_3(n):
-        tile_rows[n].wait()
-        return jnp.sum(trow[n], axis=0)
+        tile_all[n].wait()
+        return jnp.sum(tall[n], axis=0)
 
     act = fa[1:33, 0:64, :]
     tile_sums(0, act, act * act)
     ag[0:17] = conv_part(c3, w2t, 0, 17)
-    tile_sums_2(0)
     ag[17:34] = conv_part(c3, w2t, 17, 17)
-    sums = tile_sums_3(0)
+    sums = tile_sums_2(0)
     pixels = float(nr * nc * 2048)
     act_mean = sums[0:1, :] / pixels
     inverse_dev = lax.rsqrt(sums[1:2, :] / pixels - act_mean * act_mean + EPS)
@@ -576,7 +577,7 @@
         )
         for n in range(2)
     ]
-    map_sum = [to_rows(4 + n, gred.at[n], grow.at[n]) for n in range(2)]
+    map_sum = [to_rows(2 + n, gred.at[n], grow.at[n]) for n in range(2)]
     share = [
         to_chips(
             5 + n,
@@ -621,13 +622,12 @@
 
     weight_part(1, cott, a3, 0)
     grad_0(1)
-    tile_sums_2(1)
     for half in range(2):
         got = conv_part(a3, w2, 16 * half, 16)
         enh_out[16 * half : 16 * half + 16] = (
             m3[2 + 16 * half : 18 + 16 * half, 0:64, 128:256].astype(F32) + got
         ).astype(BF16)
-    sums = tile_sums_3(1)
+    sums = tile_sums_2(1)
     grad_mean = sums[0:1, :] / pixels
     cross_mean = sums[1:2, :] / pixels
     grad_1(1)
@@ -755,10 +755,8 @@
         pltpu.VMEM((3, 384, 128), BF16),
         pltpu.VMEM((34, W, 128), F32),
         pltpu.VMEM((34, W, 128), F32),
-        pltpu.VMEM((2, 8, 128), F32),
-        pltpu.VMEM((2, nc, 8, 128), F32),
-        pltpu.VMEM((2, 8, 128), F32),
-        pltpu.VMEM((2, nr, 8, 128), F32),
+        pltpu.VMEM((2, 2, 128), F32),
+        pltpu.VMEM((2, nr * nc, 2, 128), F32),
         pltpu.VMEM((2, 1152, 128), F32),
         pltpu.VMEM((2, 576, 128), F32),
         pltpu.VMEM((2, nc // 2, chunk, 128), BF16),
@@ -772,10 +770,12 @@
         dma((7,)),
         dma((7,)),
         dma((7,)),
-        dma((3,)),
-        dma((3,)),
-        dma((6,)),
-        dma((6,)),
+        dma((1,)),
+        dma((1,)),
+        dma((4,)),
+        dma((4,)),
+        dma((2,)),
+        dma((2,)),
         dma((16,)),
         dma((16,)),
     ]

time: 87.9 us -> 85.5 us (0.973)
  Pallas kernels: 87.2 us -> 84.8 us
    pallas_call x1, Pallas kernels: 85.9 us -> 83.5 us  [per_device(): pl.pallas_call(functools.partial(kernel, nr, nc), out_shape=(jax.ShapeDty...]
where the time goes in v2:
time: 85.5 us; the launch traced here: 85.4 us
  Pallas kernels  84.8 us (99%)
    pallas_call x1, Pallas kernels, per_device(): pl.pallas_call(functools.partial(kernel, nr, nc), out_shape=(jax.ShapeDty...  83.5 us

profile of v2, /device:TPU:1, one launch (start us, length us, event | category | flops | bytes accessed | tf_op | source)
XLA Modules:
  0.0 85.4 jit_solution(4595193975444010523)
XLA Ops:
  0.6 83.5 %shard_map.138 = (bf16[32,64,128]{2,1,0:T(8,128)(2,1)S(1)}, f32[1152,128]{1,0:T(8,128)S(1)}, f32[1152,128]{1,0:T(8,128)S(1)}, f32[2,4,128]{2,1,0:T(4,128)S(1)}) custom-call(bf16[128,64]{1,0:T(8,128)(2,1)} %bitcast.15, bf16[9,64,1024]{2,1,0:T(8,128)(2,1)} %bitcast.11, bf16[9,64,1024]{2,1,0:T(8,128)(2,1)} %bitcast.12, bf16[1024,128]{1,0:T(8,128)(2,1)} %pw_hbm.1, ...), custom_call_target="tpu_custom_call" | custom-call | tf_op jit(solution)/shard_map/pallas_call | solution.py:782
  84.1 1.3 %shard_map.139 = (bf16[32,64,128]{2,1,0:T(8,128)(2,1)}, f32[1152,128]{1,0:T(8,128)}, f32[1152,128]{1,0:T(8,128)}, f32[2,4,128]{2,1,0:T(4,128)}) custom-call(bf16[32,64,128]{2,1,0:T(8,128)(2,1)S(1)} %get-tuple-element.12.refs_0_, f32[1152,128]{1,0:T(8,128)S(1)} %get-tuple-element.13.refs_1_, f32[1152,128]{1,0:T(8,128)S(1)} %get-tuple-element.14.refs_2_, ...), custom_call_target="tpu_custom_call" | custom-call | tf_op jit(solution)/shard_map/pallas_call | solution.py:815

commit v3 on v2

--- a/solution.py
+++ b/solution.py
@@ -601,13 +601,13 @@
 
     def grad_2(n):
         band_sum[n].wait()
-        gred[n] = jnp.sum(gcol[n].astype(F32), axis=0)
+        gred[n] = jnp.sum(gcol[n].astype(F32), axis=0).astype(BF16)
         map_sum[n].start()
         grow[n, pl.ds(r, 1)] = gred[n][None]
 
     def grad_3(n):
         map_sum[n].wait()
-        total = jnp.sum(grow[n], axis=0)
+        total = jnp.sum(grow[n].astype(F32), axis=0)
         gfin[n] = (total * (1.0 / math.sqrt(pixels))).astype(BF16)
         share[n].start()
         gall[n, pl.ds(core, 1), pl.ds(chip, 1)] = gfin[n][None, None]
@@ -761,8 +761,8 @@
         pltpu.VMEM((2, 576, 128), F32),
         pltpu.VMEM((2, nc // 2, chunk, 128), BF16),
         pltpu.VMEM((2, nc // 2, chunk, 128), BF16),
-        pltpu.VMEM((2, chunk, 128), F32),
-        pltpu.VMEM((2, nr, chunk, 128), F32),
+        pltpu.VMEM((2, chunk, 128), BF16),
+        pltpu.VMEM((2, nr, chunk, 128), BF16),
         pltpu.VMEM((2, chunk, 128), BF16),
         pltpu.VMEM((2, 2, nc // 2, chunk, 128), BF16),
         dma((11,)),

time: 85.5 us -> 84.7 us (level)
  no operation moved by 1% of the time
where the time goes in v3:
time: 84.7 us; the launch traced here: 84.6 us
  Pallas kernels  84 us (99%)
    pallas_call x1, Pallas kernels, per_device(): pl.pallas_call(functools.partial(kernel, nr, nc), out_shape=(jax.ShapeDty...  82.7 us

profile of v3, /device:TPU:1, one launch (start us, length us, event | category | flops | bytes accessed | tf_op | source)
XLA Modules:
  0.0 84.6 jit_solution(5338633377867998236)
XLA Ops:
  0.6 82.7 %shard_map.138 = (bf16[32,64,128]{2,1,0:T(8,128)(2,1)S(1)}, f32[1152,128]{1,0:T(8,128)S(1)}, f32[1152,128]{1,0:T(8,128)S(1)}, f32[2,4,128]{2,1,0:T(4,128)S(1)}) custom-call(bf16[128,64]{1,0:T(8,128)(2,1)} %bitcast.15, bf16[9,64,1024]{2,1,0:T(8,128)(2,1)} %bitcast.11, bf16[9,64,1024]{2,1,0:T(8,128)(2,1)} %bitcast.12, bf16[1024,128]{1,0:T(8,128)(2,1)} %pw_hbm.1, ...), custom_call_target="tpu_custom_call" | custom-call | tf_op jit(solution)/shard_map/pallas_call | solution.py:782
  83.3 1.3 %shard_map.139 = (bf16[32,64,128]{2,1,0:T(8,128)(2,1)}, f32[1152,128]{1,0:T(8,128)}, f32[1152,128]{1,0:T(8,128)}, f32[2,4,128]{2,1,0:T(4,128)}) custom-call(bf16[32,64,128]{2,1,0:T(8,128)(2,1)S(1)} %get-tuple-element.12.refs_0_, f32[1152,128]{1,0:T(8,128)S(1)} %get-tuple-element.13.refs_1_, f32[1152,128]{1,0:T(8,128)S(1)} %get-tuple-element.14.refs_2_, ...), custom_call_target="tpu_custom_call" | custom-call | tf_op jit(solution)/shard_map/pallas_call | solution.py:815

commit v4 on v3

--- a/solution.py
+++ b/solution.py
@@ -630,7 +630,6 @@
     sums = tile_sums_2(1)
     grad_mean = sums[0:1, :] / pixels
     cross_mean = sums[1:2, :] / pixels
-    grad_1(1)
 
     def grad_row(i, carry):
         fg = inverse_dev * (ag[i] - grad_mean - fa[i] * cross_mean)
@@ -649,6 +648,7 @@
     lax.fori_loop(0, 4, grad_turn, 0)
     weight_part(0, fgt, m3, 1)
     grad_0(0)
+    grad_1(1)
 
     grad_1(0)
     grad_2(1)

time: 84.7 us -> 84.5 us (level)
  no operation moved by 1% of the time
where the time goes in v4:
time: 84.5 us; the launch traced here: 84.4 us
  Pallas kernels  83.8 us (99%)
    pallas_call x1, Pallas kernels, per_device(): pl.pallas_call(functools.partial(kernel, nr, nc), out_shape=(jax.ShapeDty...  82.5 us

profile of v4, /device:TPU:1, one launch (start us, length us, event | category | flops | bytes accessed | tf_op | source)
XLA Modules:
  0.0 84.4 jit_solution(6571061483188297269)
XLA Ops:
  0.6 82.5 %shard_map.138 = (bf16[32,64,128]{2,1,0:T(8,128)(2,1)S(1)}, f32[1152,128]{1,0:T(8,128)S(1)}, f32[1152,128]{1,0:T(8,128)S(1)}, f32[2,4,128]{2,1,0:T(4,128)S(1)}) custom-call(bf16[128,64]{1,0:T(8,128)(2,1)} %bitcast.15, bf16[9,64,1024]{2,1,0:T(8,128)(2,1)} %bitcast.11, bf16[9,64,1024]{2,1,0:T(8,128)(2,1)} %bitcast.12, bf16[1024,128]{1,0:T(8,128)(2,1)} %pw_hbm.1, ...), custom_call_target="tpu_custom_call" | custom-call | tf_op jit(solution)/shard_map/pallas_call | solution.py:782
  83.1 1.3 %shard_map.139 = (bf16[32,64,128]{2,1,0:T(8,128)(2,1)}, f32[1152,128]{1,0:T(8,128)}, f32[1152,128]{1,0:T(8,128)}, f32[2,4,128]{2,1,0:T(4,128)}) custom-call(bf16[32,64,128]{2,1,0:T(8,128)(2,1)S(1)} %get-tuple-element.12.refs_0_, f32[1152,128]{1,0:T(8,128)S(1)} %get-tuple-element.13.refs_1_, f32[1152,128]{1,0:T(8,128)S(1)} %get-tuple-element.14.refs_2_, ...), custom_call_target="tpu_custom_call" | custom-call | tf_op jit(solution)/shard_map/pallas_call | solution.py:815

commit v5 on v3

--- a/solution.py
+++ b/solution.py
@@ -668,6 +668,9 @@
             picked[a].append(jnp.dot(window, strip, precision=HIGH, preferred_element_type=F32))
         strip = jnp.sum(c3[UP * br + 2 : UP * br + 18, :, 128:256].astype(F32), axis=0)
         direct.append(jnp.dot(window, strip, precision=HIGH, preferred_element_type=F32)[8:16])
+    grad_2(0)
+    grad_3(1)
+
     result = jnp.concatenate(direct, axis=0)
     for a in range(3):
         for b in range(3):
@@ -678,8 +681,6 @@
     gg_out[0] = result[0:4] * (1.0 / UP)
     gg_out[1] = result[8:12] * (1.0 / UP)
 
-    grad_2(0)
-    grad_3(1)
     grad_3(0)
     grad_4(1)
     grad_4(0)

time: 84.7 us -> 84.7 us (level)
  no operation moved by 1% of the time
where the time goes in v5:
time: 84.7 us; the launch traced here: 84.6 us
  Pallas kernels  84 us (99%)
    pallas_call x1, Pallas kernels, per_device(): pl.pallas_call(functools.partial(kernel, nr, nc), out_shape=(jax.ShapeDty...  82.7 us

profile of v5, /device:TPU:1, one launch (start us, length us, event | category | flops | bytes accessed | tf_op | source)
XLA Modules:
  0.0 84.6 jit_solution(15791121365046740410)
XLA Ops:
  0.6 82.7 %shard_map.138 = (bf16[32,64,128]{2,1,0:T(8,128)(2,1)S(1)}, f32[1152,128]{1,0:T(8,128)S(1)}, f32[1152,128]{1,0:T(8,128)S(1)}, f32[2,4,128]{2,1,0:T(4,128)S(1)}) custom-call(bf16[128,64]{1,0:T(8,128)(2,1)} %bitcast.15, bf16[9,64,1024]{2,1,0:T(8,128)(2,1)} %bitcast.11, bf16[9,64,1024]{2,1,0:T(8,128)(2,1)} %bitcast.12, bf16[1024,128]{1,0:T(8,128)(2,1)} %pw_hbm.1, ...), custom_call_target="tpu_custom_call" | custom-call | tf_op jit(solution)/shard_map/pallas_call | solution.py:783
  83.3 1.3 %shard_map.139 = (bf16[32,64,128]{2,1,0:T(8,128)(2,1)}, f32[1152,128]{1,0:T(8,128)}, f32[1152,128]{1,0:T(8,128)}, f32[2,4,128]{2,1,0:T(4,128)}) custom-call(bf16[32,64,128]{2,1,0:T(8,128)(2,1)S(1)} %get-tuple-element.12.refs_0_, f32[1152,128]{1,0:T(8,128)S(1)} %get-tuple-element.13.refs_1_, f32[1152,128]{1,0:T(8,128)S(1)} %get-tuple-element.14.refs_2_, ...), custom_call_target="tpu_custom_call" | custom-call | tf_op jit(solution)/shard_map/pallas_call | solution.py:816
